TPU v7x, 128 devices: a whole 4x4x4 slice. The times are simulated.
128 devices in a mesh: obs: 8 (over z_hi, y), unk: 16 (over z_lo, x, core).
Axes of the slice: x: 4, y: 4, z: 4 (z_hi: 2, z_lo: 2; z = z_hi * 2 + z_lo), core: 2. Of those that a mesh axis runs over, the one named last changes fastest.
Arguments:
- design: float32 [8192, 24576], P('obs', 'unk'), may hold values from -0.0625 to 0.0625
- weights: float32 [8192], P('obs'), may hold values from 0.25 to 4
Outputs:
- factor: float32 [24576, 1024], P(('unk', 'obs'))
All inputs are finite; a program needn't handle non-finite values.
Results may differ from a plain program's by a relative error of at most 0.00011.
Values sent between devices are 32-bit elements; how exact they have to be, the bound alone decides.
No kernel may reach another device: no remote copies, remote signals or barrier semaphores. Data moves between devices by JAX's collectives and lax.ppermute only.
A program may use at most 128 MiB of HBM per device.

v0:
```python
import jax
import jax.numpy as jnp
from jax import lax
from jax.sharding import PartitionSpec as P

PANEL = 512
BLOCK = 128


def spread(block, axis, holder):
    block = jnp.where(lax.axis_index(axis) == holder, block, jnp.zeros_like(block))
    return lax.psum(block, axis)


def apply_lower(diag_factor, values):
    return lax.linalg.triangular_solve(
        diag_factor, values, left_side=False, lower=True, transpose_a=True
    )


def left_looking(top_block, owned_rows):
    width = top_block.shape[0]
    factor_top = jnp.zeros_like(top_block)
    factor_rows = jnp.zeros_like(owned_rows)
    for column_block in range(width // BLOCK):
        offset = column_block * BLOCK
        update_top = top_block[:, offset : offset + BLOCK]
        update_rows = owned_rows[:, offset : offset + BLOCK]
        if offset > 0:
            earlier = factor_top[offset : offset + BLOCK, :offset]
            update_top = update_top - jnp.dot(
                factor_top[:, :offset],
                earlier.T,
                precision=lax.Precision.HIGHEST,
                preferred_element_type=jnp.float32,
            )
            update_rows = update_rows - jnp.dot(
                factor_rows[:, :offset],
                earlier.T,
                precision=lax.Precision.HIGHEST,
                preferred_element_type=jnp.float32,
            )
        diag_factor = jnp.linalg.cholesky(update_top[offset : offset + BLOCK])
        below_top = apply_lower(diag_factor, update_top[offset + BLOCK :])
        new_column = jnp.concatenate(
            [jnp.zeros((offset, BLOCK), jnp.float32), diag_factor, below_top], axis=0
        )
        factor_top = factor_top.at[:, offset : offset + BLOCK].set(new_column)
        factor_rows = factor_rows.at[:, offset : offset + BLOCK].set(
            apply_lower(diag_factor, update_rows)
        )
    return factor_rows


def local(design, weights):
    panel_cols = spread(design[:, : 2 * PANEL], "unk", 0)
    weighted = panel_cols * weights[:, None]
    partial_value = lax.dot_general(
        design,
        weighted,
        (((0,), (0,)), ((), ())),
        precision=lax.Precision.HIGHEST,
        preferred_element_type=jnp.float32,
    )
    owned_rows = lax.psum_scatter(partial_value, "obs", scatter_dimension=0, tiled=True)
    gathered = lax.all_gather(owned_rows, "obs", axis=0, tiled=True)
    top_block = spread(gathered[: 2 * PANEL], "unk", 0)
    return left_looking(top_block, owned_rows)


def solution(mesh):
    return jax.shard_map(
        local,
        mesh=mesh,
        in_specs=(P("obs", "unk"), P("obs")),
        out_specs=P(("unk", "obs"), None),
        check_vma=False,
    )
```

profile of v0, /device:TPU:7, one launch (start us, length us, event | category | flops | bytes accessed | tf_op | source)
XLA Modules:
  0.0 775.2 jit_solution(10792649230344124611)
XLA Ops:
  6.5 4.7 slice.463
  11.3 5.3 copy.46
  16.6 2.8 broadcast_select_fusion.1
  19.5 132.4 %all-reduce.5.cloned.1.call-done = f32[1024,1024]{0,1:T(8,128)} async-done(((f32[1024,1024]{0,1:T(8,128)}), f32[1024,1024]{0,1:T(8,128)}) %all-reduce.5.cloned.1.call-update) | async-done | bytes 4194320 | tf_op jit(solution)/shard_map/psum | solution.py:12
  151.9 24.3 %convolution_bitcast_fusion = f32[1536,1024]{0,1:T(8,128)} fusion(f32[1024,1536]{1,0:T(8,128)} %param.35, f32[1024,1024]{0,1:T(8,128)} %all-reduce.5.cloned.1.call-done, f32[1024]{0:T(1024)S(1)} %copy-done.3), kind=kOutput, calls=%fused_computation | convolution fusion | flops 19328401408 | bytes 16781312 | tf_op jit(solution)/shard_map/dot_general | solution.py:58
  176.3 6.5 copy.44
  182.9 98.6 %reduce-scatter.4.cloned.1.call-done = f32[192,1024]{1,0:T(8,128)} async-done(((f32[1536,1024]{1,0:T(8,128)}), f32[192,1024]{1,0:T(8,128)}) %reduce-scatter.4.cloned.1.call-update) | async-done | bytes 786448 | tf_op jit(solution)/shard_map/reduce_scatter | solution.py:65
  281.5 90.1 %all-gather.2.cloned.1.call-done = f32[1536,1024]{1,0:T(8,128)} async-done(((f32[192,1024]{1,0:T(8,128)}), f32[1536,1024]{1,0:T(8,128)}) %all-gather.2.cloned.1.call-update) | async-done | bytes 6291472 | tf_op jit(solution)/shard_map/all_gather | solution.py:66
  371.6 4.7 slice.519
  376.3 5.3 copy.47
  381.7 2.8 broadcast_select_fusion
  385.9 0.7 compare_reduce_fusion.12
  388.5 1.1 compare_reduce_fusion.8
  390.4 122.7 %all-reduce.7.cloned.1.call-done = f32[1024,1024]{0,1:T(8,128)} async-done(((f32[1024,1024]{0,1:T(8,128)}), f32[1024,1024]{0,1:T(8,128)}) %all-reduce.7.cloned.1.call-update) | async-done | bytes 4194320 | tf_op jit(solution)/shard_map/psum | solution.py:12
  513.1 0.8 slice.520
  514.0 0.9 fusion.101
  514.9 11.7 %cholesky.134 = f32[128,128]{1,0:T(8,128)S(1)} custom-call(f32[128,128]{1,0:T(8,128)S(1)} %fusion.101), custom_call_target="Cholesky" | custom-call | tf_op jit(solution)/shard_map/jit(cholesky)/cholesky | solution.py:43
  527.9 9.8 %custom-call.40 = f32[1,128,128]{1,2,0:T(8,128)S(1)} custom-call(f32[1,128,128]{2,1,0:T(8,128)S(1)} %get-tuple-element.199), custom_call_target="InvertDiagBlocksLowerTriangular" | custom-call | tf_op jit(solution)/shard_map/triangular_solve/custom-call.0 | solution.py:16
  537.7 1.0 fusion.37
  538.8 2.1 fusion.48
  541.6 2.5 scatter.54
  545.2 11.9 %cholesky.145 = f32[128,128]{1,0:T(8,128)S(1)} custom-call(f32[128,128]{1,0:T(8,128)S(1)} %fusion.98), custom_call_target="Cholesky" | custom-call | tf_op jit(solution)/shard_map/jit(cholesky)/cholesky | solution.py:43
  558.4 9.8 %custom-call.41 = f32[1,128,128]{1,2,0:T(8,128)S(1)} custom-call(f32[1,128,128]{2,1,0:T(8,128)S(1)} %get-tuple-element.197), custom_call_target="InvertDiagBlocksLowerTriangular" | custom-call | tf_op jit(solution)/shard_map/triangular_solve/custom-call.0 | solution.py:16
  568.2 0.8 fusion.53
  569.1 1.5 fusion.46
  570.6 2.6 convolution_subtract_fusion
  573.4 11.7 %cholesky.156 = f32[128,128]{1,0:T(8,128)S(1)} custom-call(f32[128,128]{1,0:T(8,128)S(1)} %fusion.95), custom_call_target="Cholesky" | custom-call | tf_op jit(solution)/shard_map/jit(cholesky)/cholesky | solution.py:43
  586.4 9.8 %custom-call.42 = f32[1,128,128]{1,2,0:T(8,128)S(1)} custom-call(f32[1,128,128]{2,1,0:T(8,128)S(1)} %get-tuple-element.195), custom_call_target="InvertDiagBlocksLowerTriangular" | custom-call | tf_op jit(solution)/shard_map/triangular_solve/custom-call.0 | solution.py:16
  596.2 0.7 fusion.57
  596.9 1.0 fusion.36
  597.9 1.3 convolution_subtract_fusion.8
  599.2 1.2 fusion.34
  600.4 2.7 fusion.45
  603.1 3.4 fusion.15
  606.6 11.7 %cholesky.167 = f32[128,128]{1,0:T(8,128)S(1)} custom-call(f32[128,128]{1,0:T(8,128)S(1)} %fusion.92), custom_call_target="Cholesky" | custom-call | tf_op jit(solution)/shard_map/jit(cholesky)/cholesky | solution.py:43
  619.7 9.8 %custom-call.43 = f32[1,128,128]{1,2,0:T(8,128)S(1)} custom-call(f32[1,128,128]{2,1,0:T(8,128)S(1)} %get-tuple-element.193), custom_call_target="InvertDiagBlocksLowerTriangular" | custom-call | tf_op jit(solution)/shard_map/triangular_solve/custom-call.0 | solution.py:16
  630.1 1.5 convolution_subtract_fusion.5
  631.6 1.0 fusion.32
  632.6 2.7 fusion.44
  635.3 4.0 fusion.21
  639.5 12.1 %cholesky.178 = f32[128,128]{1,0:T(8,128)S(1)} custom-call(f32[128,128]{1,0:T(8,128)S(1)} %fusion.89), custom_call_target="Cholesky" | custom-call | tf_op jit(solution)/shard_map/jit(cholesky)/cholesky | solution.py:43
  652.9 9.8 %custom-call.44 = f32[1,128,128]{1,2,0:T(8,128)S(1)} custom-call(f32[1,128,128]{2,1,0:T(8,128)S(1)} %get-tuple-element.191), custom_call_target="InvertDiagBlocksLowerTriangular" | custom-call | tf_op jit(solution)/shard_map/triangular_solve/custom-call.0 | solution.py:16
  663.2 1.5 convolution_subtract_fusion.4
  664.7 1.0 fusion.30
  665.7 2.7 fusion.43
  668.3 4.7 fusion.18
  673.2 11.8 %cholesky.189 = f32[128,128]{1,0:T(8,128)S(1)} custom-call(f32[128,128]{1,0:T(8,128)S(1)} %fusion.86), custom_call_target="Cholesky" | custom-call | tf_op jit(solution)/shard_map/jit(cholesky)/cholesky | solution.py:43
  686.4 9.8 %custom-call.45 = f32[1,128,128]{1,2,0:T(8,128)S(1)} custom-call(f32[1,128,128]{2,1,0:T(8,128)S(1)} %get-tuple-element.189), custom_call_target="InvertDiagBlocksLowerTriangular" | custom-call | tf_op jit(solution)/shard_map/triangular_solve/custom-call.0 | solution.py:16
  696.6 1.7 convolution_subtract_fusion.3
  698.2 1.0 fusion.28
  699.2 2.7 fusion.42
  702.0 5.4 fusion.12
  707.5 11.7 %cholesky.200 = f32[128,128]{1,0:T(8,128)S(1)} custom-call(f32[128,128]{1,0:T(8,128)S(1)} %fusion.83), custom_call_target="Cholesky" | custom-call | tf_op jit(solution)/shard_map/jit(cholesky)/cholesky | solution.py:43
  720.6 10.0 %custom-call.46 = f32[1,128,128]{1,2,0:T(8,128)S(1)} custom-call(f32[1,128,128]{2,1,0:T(8,128)S(1)} %get-tuple-element.187), custom_call_target="InvertDiagBlocksLowerTriangular" | custom-call | tf_op jit(solution)/shard_map/triangular_solve/custom-call.0 | solution.py:16
  730.9 1.8 convolution_subtract_fusion.2
  732.7 0.9 fusion.26
  733.7 2.6 fusion.41
  736.3 6.0 fusion.1
  742.4 11.7 %cholesky.211 = f32[128,128]{1,0:T(8,128)S(1)} custom-call(f32[128,128]{1,0:T(8,128)S(1)} %fusion.80), custom_call_target="Cholesky" | custom-call | tf_op jit(solution)/shard_map/jit(cholesky)/cholesky | solution.py:43
  754.2 0.7 compare_reduce_fusion
  754.9 0.7 fusion.76
  755.6 9.8 %custom-call.47 = f32[1,128,128]{1,2,0:T(8,128)S(1)} custom-call(f32[1,128,128]{2,1,0:T(8,128)S(1)} %fusion.76), custom_call_target="InvertDiagBlocksLowerTriangular" | custom-call | tf_op jit(solution)/shard_map/triangular_solve/custom-call.0 | solution.py:16
  765.4 1.9 convolution_subtract_fusion.6
  767.4 1.0 fusion.24
  (94 shorter events, 17.9 us)
Async XLA Ops:
  6.5 145.4 %all-reduce.5.cloned.1.call-start = ((), (), s32[]{:S(2)}) async-start(), calls=%async_computation.1 | async-start | bytes 8388608 | tf_op jit(solution)/shard_map/psum | solution.py:12
  19.4 132.5 %copy-start.3 = (f32[1024]{0:T(1024)S(1)}, f32[1024]{0:T(1024)}, u32[]{:S(2)}) copy-start(f32[1024]{0:T(1024)} %param.36) | copy-start | bytes 12292
  19.4 262.0 %reduce-scatter.4.cloned.1.call-start = ((), (), s32[]{:S(2)}) async-start(), calls=%async_computation.4 | async-start | bytes 7077888 | tf_op jit(solution)/shard_map/reduce_scatter | solution.py:65
  182.8 188.8 %all-gather.2.cloned.1.call-start = ((), (), s32[]{:S(2)}) async-start(), calls=%async_computation.2 | async-start | bytes 7077888 | tf_op jit(solution)/shard_map/all_gather | solution.py:66
  281.5 231.6 %all-reduce.7.cloned.1.call-start = ((), (), s32[]{:S(2)}) async-start(), calls=%async_computation.3 | async-start | bytes 8388608 | tf_op jit(solution)/shard_map/psum | solution.py:12
  384.5 5.1 copy-start.2
  537.7 6.7 copy-start.1
  730.9 11.4 %slice-start = ((f32[1024,1024]{0,1:T(8,128)}), f32[1024,128]{0,1:T(8,128)S(1)}, s32[]{:S(2)}) async-start(f32[1024,1024]{0,1:T(8,128)} %all-reduce.7.cloned.1.call-done), calls=%async_computation.5 | async-start | bytes 1048576 | tf_op jit(solution)/shard_map/slice | solution.py:27
  733.6 33.7 %copy-start = (f32[192,1024]{1,0:T(8,128)}, f32[192,1024]{1,0:T(8,128)S(1)}, u32[]{:S(2)}) copy-start(f32[192,1024]{1,0:T(8,128)S(1)} %fusion.26) | copy-start | bytes 2359300
Sparse Core Ops, SparseCore 0:
  19.5 132.3 all-reduce.4
  182.9 98.4 reduce-scatter.3
  283.7 87.8 all-gather.1
  384.6 128.3 all-reduce.6
where the time goes:
time: 783 us; the launch traced here: 775 us
  waiting for transfers between devices  444 us (57%)
  other arithmetic  211 us (27%)
  matrix products  74.5 us (10%)
  local copies, waits for them, and re-layouts  31.6 us (4%)
  between operations  14.1 us (2%)
    psum x2, waiting for transfers between devices, spread(): return lax.psum(block, axis)  255 us
    another operation x24, other arithmetic, left_looking(): diag_factor = jnp.linalg.cholesky(update_top[offset:offset + BLOCK])  99.8 us
    reduce_scatter x1, waiting for transfers between devices, local(): lax.psum_scatter(partial_value, 'obs', scatter_dimension=0, tiled=True)  98.6 us
    all_gather x1, waiting for transfers between devices, local(): gathered = lax.all_gather(owned_rows, 'obs', axis=0, tiled=True)  90.1 us
    another operation x16, other arithmetic, apply_lower(): lax.linalg.triangular_solve(diag_factor, values, left_side=False, lower=T...  84 us
    dot_general x7, matrix products, left_looking(): jnp.dot(factor_top[:, :offset], earlier.T, precision=lax.Precision.HIGHES...  26.8 us
    dot_general x1, matrix products, local(): lax.dot_general(design, weighted, (((0,), (0,)), ((), ())), precision=lax...  24.3 us
    unnamed x18, local copies, waits for them, and re-layouts  17.9 us
  transfers between devices with their start and end apart: 4, of which 4 were waited for; matrix products, arithmetic and copies ran while one was open for 1% of the time, Pallas kernels for 0%

commit v1 on v0

--- a/solution.py
+++ b/solution.py
@@ -63,7 +63,9 @@
         preferred_element_type=jnp.float32,
     )
     owned_rows = lax.psum_scatter(partial_value, "obs", scatter_dimension=0, tiled=True)
-    gathered = lax.all_gather(owned_rows, "obs", axis=0, tiled=True)
+    gathered = jnp.concatenate(
+        lax.all_to_all(jnp.stack([owned_rows] * lax.axis_size("obs")), "obs", 0, 0), axis=0
+    )
     top_block = spread(gathered[: 2 * PANEL], "unk", 0)
     return left_looking(top_block, owned_rows)
 

time: 783 us -> 767 us (0.980)
  waiting for transfers between devices: 444 us -> 357 us
  blocking collectives: 0 us -> 73.6 us
    all_gather x1 -> x0, waiting for transfers between devices: 90.1 us -> none  [local(): gathered = lax.all_gather(owned_rows, 'obs', axis=0, tiled=True)]
    all_to_all x0 -> x1, blocking collectives: none -> 73.6 us  [local(): lax.all_to_all(jnp.stack([owned_rows] * lax.axis_size('obs')), 'obs', 0, 0)]
    unnamed x18 -> x11, local copies, waits for them, and re-layouts: 17.9 us -> 17.2 us
  transfers between devices with their start and end apart: 4 -> 3, of which waited for: 4 -> 3; matrix products, arithmetic and copies ran while one was open for 1% -> 1% of each run, Pallas kernels for 0% -> 0%
where the time goes in v1:
time: 767 us; the launch traced here: 759 us
  waiting for transfers between devices  357 us (47%)
  other arithmetic  211 us (28%)
  blocking collectives  73.6 us (10%)
  matrix products  73.2 us (10%)
  local copies, waits for them, and re-layouts  30.4 us (4%)
  between operations  14 us (2%)
    psum x2, waiting for transfers between devices, spread(): return lax.psum(block, axis)  258 us
    another operation x24, other arithmetic, left_looking(): diag_factor = jnp.linalg.cholesky(update_top[offset:offset + BLOCK])  99.7 us
    reduce_scatter x1, waiting for transfers between devices, local(): lax.psum_scatter(partial_value, 'obs', scatter_dimension=0, tiled=True)  98.6 us
    another operation x16, other arithmetic, apply_lower(): lax.linalg.triangular_solve(diag_factor, values, left_side=False, lower=T...  83.9 us
    all_to_all x1, blocking collectives, local(): lax.all_to_all(jnp.stack([owned_rows] * lax.axis_size('obs')), 'obs', 0, 0)  73.6 us
    dot_general x7, matrix products, left_looking(): jnp.dot(factor_top[:, :offset], earlier.T, precision=lax.Precision.HIGHES...  27.1 us
    dot_general x1, matrix products, local(): lax.dot_general(design, weighted, (((0,), (0,)), ((), ())), precision=lax...  24.3 us
    unnamed x11, local copies, waits for them, and re-layouts  17.2 us
  transfers between devices with their start and end apart: 3, of which 3 were waited for; matrix products, arithmetic and copies ran while one was open for 1% of the time, Pallas kernels for 0%

profile of v1, /device:TPU:7, one launch (start us, length us, event | category | flops | bytes accessed | tf_op | source)
XLA Modules:
  0.0 758.7 jit_solution(7355347581811947366)
XLA Ops:
  6.5 4.7 slice.463
  11.3 5.3 copy.71
  16.6 2.8 broadcast_select_fusion.1
  19.5 132.4 %all-reduce.5.cloned.1.call-done = f32[1024,1024]{0,1:T(8,128)} async-done(((f32[1024,1024]{0,1:T(8,128)}), f32[1024,1024]{0,1:T(8,128)}) %all-reduce.5.cloned.1.call-update) | async-done | bytes 4194320 | tf_op jit(solution)/shard_map/psum | solution.py:12
  151.9 24.3 %convolution_bitcast_fusion = f32[1536,1024]{0,1:T(8,128)} fusion(f32[1024,1536]{1,0:T(8,128)} %param.35, f32[1024,1024]{0,1:T(8,128)} %all-reduce.5.cloned.1.call-done, f32[1024]{0:T(1024)S(1)} %copy-done.3), kind=kOutput, calls=%fused_computation | convolution fusion | flops 19328401408 | bytes 16781312 | tf_op jit(solution)/shard_map/dot_general | solution.py:58
  176.3 6.5 copy.69
  182.9 98.6 %reduce-scatter.4.cloned.1.call-done = f32[192,1024]{1,0:T(8,128)} async-done(((f32[1536,1024]{1,0:T(8,128)}), f32[192,1024]{1,0:T(8,128)}) %reduce-scatter.4.cloned.1.call-update) | async-done | bytes 786448 | tf_op jit(solution)/shard_map/reduce_scatter | solution.py:65
  281.4 1.9 stack.2
  283.3 73.6 %all_to_all.5 = f32[8,192,1024]{2,1,0:T(8,128)S(1)} all-to-all(f32[8,192,1024]{2,1,0:T(8,128)S(1)} %stack.2), channel_id=1, replica_groups=mesh['obs'=8,'unk'=16] {'obs'}, dimensions={0} | all-to-all | bytes 12582912 | tf_op jit(solution)/shard_map/all_to_all | solution.py:67
  356.9 2.2 slice.519
  359.1 5.3 copy.72
  364.5 2.8 broadcast_select_fusion
  371.2 1.1 compare_reduce_fusion.8
  372.3 125.9 %all-reduce.7.cloned.1.call-done = f32[1024,1024]{0,1:T(8,128)} async-done(((f32[1024,1024]{0,1:T(8,128)}), f32[1024,1024]{0,1:T(8,128)}) %all-reduce.7.cloned.1.call-update) | async-done | bytes 4194320 | tf_op jit(solution)/shard_map/psum | solution.py:12
  498.2 0.8 slice.520
  499.1 0.9 fusion.101
  500.0 11.7 %cholesky.134 = f32[128,128]{1,0:T(8,128)S(1)} custom-call(f32[128,128]{1,0:T(8,128)S(1)} %fusion.101), custom_call_target="Cholesky" | custom-call | tf_op jit(solution)/shard_map/jit(cholesky)/cholesky | solution.py:43
  513.1 9.8 %custom-call.40 = f32[1,128,128]{1,2,0:T(8,128)S(1)} custom-call(f32[1,128,128]{2,1,0:T(8,128)S(1)} %get-tuple-element.199), custom_call_target="InvertDiagBlocksLowerTriangular" | custom-call | tf_op jit(solution)/shard_map/triangular_solve/custom-call.0 | solution.py:16
  522.9 1.0 fusion.37
  524.0 2.1 fusion.48
  526.7 2.5 scatter.54
  530.0 11.7 %cholesky.145 = f32[128,128]{1,0:T(8,128)S(1)} custom-call(f32[128,128]{1,0:T(8,128)S(1)} %fusion.98), custom_call_target="Cholesky" | custom-call | tf_op jit(solution)/shard_map/jit(cholesky)/cholesky | solution.py:43
  541.8 0.8 compare_reduce_fusion.6
  543.2 9.8 %custom-call.41 = f32[1,128,128]{1,2,0:T(8,128)S(1)} custom-call(f32[1,128,128]{2,1,0:T(8,128)S(1)} %get-tuple-element.197), custom_call_target="InvertDiagBlocksLowerTriangular" | custom-call | tf_op jit(solution)/shard_map/triangular_solve/custom-call.0 | solution.py:16
  553.0 0.8 fusion.53
  553.9 1.5 fusion.46
  555.4 2.6 convolution_subtract_fusion
  558.2 11.7 %cholesky.156 = f32[128,128]{1,0:T(8,128)S(1)} custom-call(f32[128,128]{1,0:T(8,128)S(1)} %fusion.95), custom_call_target="Cholesky" | custom-call | tf_op jit(solution)/shard_map/jit(cholesky)/cholesky | solution.py:43
  571.2 9.8 %custom-call.42 = f32[1,128,128]{1,2,0:T(8,128)S(1)} custom-call(f32[1,128,128]{2,1,0:T(8,128)S(1)} %get-tuple-element.195), custom_call_target="InvertDiagBlocksLowerTriangular" | custom-call | tf_op jit(solution)/shard_map/triangular_solve/custom-call.0 | solution.py:16
  582.0 0.9 fusion.36
  582.9 1.2 convolution_subtract_fusion.8
  584.1 0.8 fusion.34
  584.9 2.6 fusion.45
  587.5 3.6 fusion.15
  591.3 11.7 %cholesky.167 = f32[128,128]{1,0:T(8,128)S(1)} custom-call(f32[128,128]{1,0:T(8,128)S(1)} %fusion.92), custom_call_target="Cholesky" | custom-call | tf_op jit(solution)/shard_map/jit(cholesky)/cholesky | solution.py:43
  604.3 9.8 %custom-call.43 = f32[1,128,128]{1,2,0:T(8,128)S(1)} custom-call(f32[1,128,128]{2,1,0:T(8,128)S(1)} %get-tuple-element.193), custom_call_target="InvertDiagBlocksLowerTriangular" | custom-call | tf_op jit(solution)/shard_map/triangular_solve/custom-call.0 | solution.py:16
  614.7 1.4 convolution_subtract_fusion.7
  616.1 0.9 fusion.32
  617.0 2.7 fusion.44
  619.7 4.0 fusion.21
  623.9 12.1 %cholesky.178 = f32[128,128]{1,0:T(8,128)S(1)} custom-call(f32[128,128]{1,0:T(8,128)S(1)} %fusion.89), custom_call_target="Cholesky" | custom-call | tf_op jit(solution)/shard_map/jit(cholesky)/cholesky | solution.py:43
  637.3 9.8 %custom-call.44 = f32[1,128,128]{1,2,0:T(8,128)S(1)} custom-call(f32[1,128,128]{2,1,0:T(8,128)S(1)} %get-tuple-element.191), custom_call_target="InvertDiagBlocksLowerTriangular" | custom-call | tf_op jit(solution)/shard_map/triangular_solve/custom-call.0 | solution.py:16
  647.6 1.4 convolution_subtract_fusion.5
  649.1 0.8 fusion.30
  649.9 2.7 fusion.43
  652.6 4.7 fusion.18
  657.5 11.7 %cholesky.189 = f32[128,128]{1,0:T(8,128)S(1)} custom-call(f32[128,128]{1,0:T(8,128)S(1)} %fusion.86), custom_call_target="Cholesky" | custom-call | tf_op jit(solution)/shard_map/jit(cholesky)/cholesky | solution.py:43
  670.5 9.9 %custom-call.45 = f32[1,128,128]{1,2,0:T(8,128)S(1)} custom-call(f32[1,128,128]{2,1,0:T(8,128)S(1)} %get-tuple-element.189), custom_call_target="InvertDiagBlocksLowerTriangular" | custom-call | tf_op jit(solution)/shard_map/triangular_solve/custom-call.0 | solution.py:16
  680.8 1.6 convolution_subtract_fusion.4
  682.4 0.9 fusion.28
  683.3 2.7 fusion.42
  686.0 5.4 fusion.12
  691.6 11.7 %cholesky.200 = f32[128,128]{1,0:T(8,128)S(1)} custom-call(f32[128,128]{1,0:T(8,128)S(1)} %fusion.83), custom_call_target="Cholesky" | custom-call | tf_op jit(solution)/shard_map/jit(cholesky)/cholesky | solution.py:43
  704.7 9.8 %custom-call.46 = f32[1,128,128]{1,2,0:T(8,128)S(1)} custom-call(f32[1,128,128]{2,1,0:T(8,128)S(1)} %get-tuple-element.187), custom_call_target="InvertDiagBlocksLowerTriangular" | custom-call | tf_op jit(solution)/shard_map/triangular_solve/custom-call.0 | solution.py:16
  714.8 1.9 convolution_subtract_fusion.3
  716.7 0.8 fusion.26
  717.5 2.6 fusion.41
  720.2 6.0 fusion.1
  726.3 11.7 %cholesky.211 = f32[128,128]{1,0:T(8,128)S(1)} custom-call(f32[128,128]{1,0:T(8,128)S(1)} %fusion.80), custom_call_target="Cholesky" | custom-call | tf_op jit(solution)/shard_map/jit(cholesky)/cholesky | solution.py:43
  738.1 0.7 compare_reduce_fusion
  738.8 0.7 fusion.76
  739.5 9.8 %custom-call.47 = f32[1,128,128]{1,2,0:T(8,128)S(1)} custom-call(f32[1,128,128]{2,1,0:T(8,128)S(1)} %fusion.76), custom_call_target="InvertDiagBlocksLowerTriangular" | custom-call | tf_op jit(solution)/shard_map/triangular_solve/custom-call.0 | solution.py:16
  749.3 1.8 convolution_subtract_fusion.2
  751.1 0.9 fusion.24
  (85 shorter events, 17.8 us)
Async XLA Ops:
  6.5 145.4 %all-reduce.5.cloned.1.call-start = ((), (), s32[]{:S(2)}) async-start(), calls=%async_computation.2 | async-start | bytes 8388608 | tf_op jit(solution)/shard_map/psum | solution.py:12
  19.4 132.5 %copy-start.3 = (f32[1024]{0:T(1024)S(1)}, f32[1024]{0:T(1024)}, u32[]{:S(2)}) copy-start(f32[1024]{0:T(1024)} %param.36) | copy-start | bytes 12292
  19.4 262.0 %reduce-scatter.4.cloned.1.call-start = ((), (), s32[]{:S(2)}) async-start(), calls=%async_computation.4 | async-start | bytes 7077888 | tf_op jit(solution)/shard_map/reduce_scatter | solution.py:65
  182.8 315.4 %all-reduce.7.cloned.1.call-start = ((), (), s32[]{:S(2)}) async-start(), calls=%async_computation.3 | async-start | bytes 8388608 | tf_op jit(solution)/shard_map/psum | solution.py:12
  367.3 155.6 %copy-start.2 = (f32[192,1024]{1,0:T(8,128)S(1)}, f32[192,1024]{1,0:T(8,128)}, u32[]{:S(2)}) copy-start(f32[192,1024]{1,0:T(8,128)} %reduce-scatter.4.cloned.1.call-done) | copy-start | bytes 2359300
  522.9 6.3 copy-start.1
  714.8 11.4 %slice-start = ((f32[1024,1024]{0,1:T(8,128)}), f32[1024,128]{0,1:T(8,128)S(1)}, s32[]{:S(2)}) async-start(f32[1024,1024]{0,1:T(8,128)} %all-reduce.7.cloned.1.call-done), calls=%async_computation.5 | async-start | bytes 1048576 | tf_op jit(solution)/shard_map/slice | solution.py:27
  717.5 33.6 %copy-start = (f32[192,1024]{1,0:T(8,128)}, f32[192,1024]{1,0:T(8,128)S(1)}, u32[]{:S(2)}) copy-start(f32[192,1024]{1,0:T(8,128)S(1)} %fusion.26) | copy-start | bytes 2359300
Sparse Core Ops, SparseCore 0:
  19.5 132.3 all-reduce.4
  182.9 98.4 reduce-scatter.3
  367.4 130.7 all-reduce.6
